TPU v7x, 512 devices: a whole 4x4x16 slice. The times are simulated.
512 devices in a mesh: seq: 64 (over x, z), chan: 8 (over y, core).
Axes of the slice: x: 4, y: 4, z: 16, core: 2. Of those that a mesh axis runs over, the one named last changes fastest.
Arguments:
- key_gate: bfloat16 [16384, 8192], P('seq', 'chan'), may hold values from -6 to 6
- values: bfloat16 [16384, 8192], P('seq', 'chan'), may hold values from -6 to 6
- query_gate: bfloat16 [16384, 8192], P('seq', 'chan'), may hold values from -6 to 6
- grad_output: bfloat16 [16384, 8192], P(('seq', 'chan')), may hold values from -6 to 6
- short_taps: bfloat16 [7, 8192], P(None, 'chan'), may hold values from -2 to 2
- long_taps: bfloat16 [128, 8192], P(None, 'chan'), may hold values from -0.5 to 0.5
Outputs:
- grad_query: bfloat16 [16384, 8192], P('seq', 'chan')
- grad_key: bfloat16 [16384, 8192], P('seq', 'chan')
- grad_value: bfloat16 [16384, 8192], P('seq', 'chan')
- grad_long: float32 [128, 8192], P('seq', 'chan')
- grad_short: float32 [7, 8192], P(None, 'chan')
All inputs are finite; a program needn't handle non-finite values.
Results may differ from a plain program's by a relative error of at most 0.0059.
Values may be sent and summed in bfloat16 or wider, within the bound.
A program may use at most 64 MiB of HBM per device.

v0:
```python
import jax
import jax.numpy as jnp
from jax import lax
from jax.sharding import PartitionSpec as P


def passed_along(shard, axis, by):
    length = lax.axis_size(axis)
    pairs = [(i, i + by) for i in range(length) if 0 <= i + by < length]
    return lax.ppermute(shard, axis, pairs)


def depthwise(extended, kernel):
    channels = kernel.shape[2]
    result = lax.conv_general_dilated(
        extended[None],
        kernel,
        (1,),
        [(0, 0)],
        dimension_numbers=("NWC", "WIO", "NWC"),
        feature_group_count=channels,
        preferred_element_type=jnp.float32,
    )
    return result[0]


def causal_apply(extended, weights):
    return depthwise(extended, jnp.flip(weights, 0)[:, None, :])


def forward_apply(extended, weights):
    return depthwise(extended, weights[:, None, :])


def filter_partial(history, grad):
    return jnp.flip(depthwise(history, grad[:, None, :]), 0)


def body(key_gate, values, query_gate, grad_output, short_taps, long_taps):
    long_len = long_taps.shape[0]
    short_len = short_taps.shape[0]
    row_count = key_gate.shape[0]
    cotangent = lax.all_to_all(grad_output, "chan", split_axis=1, concat_axis=0, tiled=True)
    product = (key_gate.astype(jnp.float32) * values.astype(jnp.float32)).astype(jnp.bfloat16)
    grad_mixed = (cotangent.astype(jnp.float32) * query_gate.astype(jnp.float32)).astype(
        jnp.bfloat16
    )
    short_hist = passed_along(product[row_count - (short_len - 1) :], "seq", 1)
    short_ext = jnp.concatenate([short_hist, product], 0)
    short_out = causal_apply(short_ext, short_taps).astype(jnp.bfloat16)
    long_hist = passed_along(short_out[row_count - (long_len - 1) :], "seq", 1)
    long_ext = jnp.concatenate([long_hist, short_out], 0)
    head_long = passed_along(grad_mixed[: long_len - 1], "seq", -1)
    long_back = jnp.concatenate([grad_mixed, head_long], 0)
    grad_conv = forward_apply(long_back, long_taps).astype(jnp.bfloat16)
    head_short = passed_along(grad_conv[: short_len - 1], "seq", -1)
    short_back = jnp.concatenate([grad_conv, head_short], 0)
    mixed = causal_apply(long_ext, long_taps)
    grad_query = (cotangent.astype(jnp.float32) * mixed).astype(jnp.bfloat16)
    grad_product = forward_apply(short_back, short_taps)
    grad_key = (grad_product * values.astype(jnp.float32)).astype(jnp.bfloat16)
    grad_value = (grad_product * key_gate.astype(jnp.float32)).astype(jnp.bfloat16)
    long_part = filter_partial(long_ext, grad_mixed)
    short_part = filter_partial(short_ext, grad_conv)
    grad_long = lax.psum_scatter(long_part, "seq", scatter_dimension=0, tiled=True)
    grad_short = lax.psum(short_part, "seq")
    return (grad_query, grad_key, grad_value, grad_long, grad_short)


def solution(mesh):
    in_specs = (
        P("seq", "chan"),
        P("seq", "chan"),
        P("seq", "chan"),
        P(("seq", "chan"), None),
        P(None, "chan"),
        P(None, "chan"),
    )
    out_specs = (
        P("seq", "chan"),
        P("seq", "chan"),
        P("seq", "chan"),
        P("seq", "chan"),
        P(None, "chan"),
    )
    return jax.shard_map(body, mesh=mesh, in_specs=in_specs, out_specs=out_specs, check_vma=False)
```

profile of v0, /device:TPU:24, one launch (start us, length us, event | category | flops | bytes accessed | tf_op | source)
XLA Modules:
  0.0 632.5 jit_solution(11481029039536911054)
XLA Ops:
  7.2 1.1 copy.87
  8.4 16.3 %all_to_all.13 = bf16[32,8,1024]{2,0,1:T(8,128)(2,1)S(1)} all-to-all(bf16[32,8,1024]{2,0,1:T(8,128)(2,1)S(1)} %bitcast.63), channel_id=1, replica_groups=mesh['seq'=64,'chan'=8] {'chan'}, dimensions={1} | all-to-all | bytes 1048576 | tf_op jit(solution)/shard_map/all_to_all | solution.py:43
  24.9 1.4 collective-permute-start.2
  26.4 8.3 %collective-permute-done.2 = bf16[127,1024]{1,0:T(8,128)(2,1)S(1)} collective-permute-done((bf16[127,1024]{1,0:T(8,128)(2,1)S(1)}, bf16[127,1024]{1,0:T(8,128)(2,1)S(1)}, u32[]{:S(2)}, u32[]{:S(2)}) %collective-permute-start.2) | collective-permute-done | bytes 260128 | tf_op jit(solution)/shard_map/ppermute | solution.py:10
  34.7 14.2 %fusion.2 = bf16[1,256,1024]{2,0,1:T(2,128)(2,1)S(1)} fusion(bf16[1,383,1024]{2,1,0:T(8,128)(2,1)S(1)} %maximum_bitcast_fusion.1, bf16[128,1,1024]{2,0,1:T(8,128)(2,1)S(1)} %bitcast.65), kind=kOutput, calls=%fused_computation.4 | convolution fusion | flops 67371008 | bytes 1570816 | tf_op jit(solution)/shard_map/conv_general_dilated | solution.py:15
  48.9 1.3 collective-permute-start.3
  50.4 4.2 collective-permute-done.3
  54.9 0.3 copy.48
  55.4 0.6 convolution_select_fusion
  56.0 0.6 copy.50
  56.8 2.6 fusion.14
  59.4 1.8 collective-permute-start
  61.5 2.6 rev.17
  64.1 1.3 dynamic-slice
  66.1 2.5 fusion.12
  69.5 0.6 fusion.5
  70.7 3.8 collective-permute-start.1
  74.5 278.3 %psum.7 = f32[7,1024]{1,0:T(8,128)} all-reduce(f32[7,1024]{1,0:T(8,128)S(1)} %rev.19), channel_id=1, replica_groups=mesh['seq'=64,'chan'=8] {'seq'}, use_global_device_ids=true, to_apply=%region_1.2 | all-reduce | flops 7168 | bytes 57344 | tf_op jit(solution)/shard_map/psum | solution.py:66
  353.1 13.9 %fusion.8 = f32[1,128,1024]{2,0,1:T(1,128)S(1)} fusion(bf16[1,383,1024]{2,1,0:T(8,128)(2,1)S(1)} %maximum_bitcast_fusion, bf16[256,1,1024]{2,0,1:T(8,128)(2,1)S(1)} %bitcast.60), kind=kOutput, calls=%fused_computation.12 | convolution fusion | flops 67108864 | bytes 1832960 | tf_op jit(solution)/shard_map/conv_general_dilated | solution.py:15
  367.1 2.7 rev.18
  369.8 14.2 %fusion.10 = f32[1,256,1024]{2,0,1:T(1,128)S(1)} fusion(bf16[1,383,1024]{2,1,0:T(8,128)(2,1)S(1)} %maximum_bitcast_fusion, bf16[128,1,1024]{2,0,1:T(8,128)(2,1)S(1)} %bitcast.66), kind=kOutput, calls=%fused_computation.14 | convolution fusion | flops 67108864 | bytes 2095104 | tf_op jit(solution)/shard_map/conv_general_dilated | solution.py:15
  384.0 1.1 fusion.17
  385.0 239.2 %all-reduce.3.cloned.1.call-done = f32[128,1024]{1,0:T(8,128)} async-done(((f32[128,1024]{1,0:T(8,128)}), f32[128,1024]{1,0:T(8,128)}) %all-reduce.3.cloned.1.call-update) | async-done | bytes 524304
  624.3 1.4 constant_dynamic-slice_fusion
  (46 shorter events, 3.1 us)
Async XLA Ops:
  7.2 17.5 %copy-start.2 = (bf16[256,1024]{1,0:T(8,128)(2,1)S(1)}, bf16[256,1024]{1,0:T(8,128)(2,1)}, u32[]{:S(2)}) copy-start(bf16[256,1024]{1,0:T(8,128)(2,1)} %param.8) | copy-start | bytes 1572868
  7.2 617.1 %all-reduce.3.cloned.1.call-start = ((), (), s32[]{:S(2)}) async-start(), calls=%async_computation.1 | async-start | bytes 1048576
  24.9 9.8 %copy-start.3 = (bf16[128,1024]{1,0:T(8,128)(2,1)S(1)}, bf16[128,1024]{1,0:T(8,128)(2,1)}, u32[]{:S(2)}) copy-start(bf16[128,1024]{1,0:T(8,128)(2,1)} %param.11) | copy-start | bytes 786436
  24.9 9.7 %collective-permute-start.2 = (bf16[127,1024]{1,0:T(8,128)(2,1)S(1)}, bf16[127,1024]{1,0:T(8,128)(2,1)S(1)}, u32[]{:S(2)}, u32[]{:S(2)}) collective-permute-start(bf16[127,1024]{1,0:T(8,128)(2,1)S(1)} %slice.33), channel_id=1, source_target_pairs={{8,0},{16,8},{24,16},{32,24},{40,32},{48,40},{56,48},{64,56},{72,6... | collective-permute-start | bytes 780296 | tf_op jit(solution)/shard_map/ppermute | solution.py:10
  48.9 5.7 copy-start
  48.9 5.6 collective-permute-start.3
  54.7 0.7 copy-start.6
  54.7 0.7 copy-start.7
  56.8 4.7 copy-start.4
  59.4 6.7 %copy-start.1 = (bf16[1,256,1024]{2,0,1:T(2,128)(2,1)S(1)}, bf16[1,256,1024]{2,0,1:T(2,128)(2,1)}, u32[]{:S(2)}) copy-start(bf16[1,256,1024]{2,0,1:T(2,128)(2,1)} %copy-done) | copy-start | bytes 1572868
  59.4 6.6 %collective-permute-start = (bf16[6,1024]{1,0:T(8,128)(2,1)S(1)}, bf16[6,1024]{1,0:T(8,128)(2,1)S(1)}, u32[]{:S(2)}, u32[]{:S(2)}) collective-permute-start(bf16[6,1024]{1,0:T(8,128)(2,1)S(1)} %slice.29), channel_id=1, source_target_pairs={{0,8},{8,16},{16,24},{24,32},{32,40},{40,48},{48,56},{56,64},{64,7... | collective-permute-start | bytes 36872 | tf_op jit(solution)/shard_map/ppermute | solution.py:10
  70.7 282.2 %collective-permute-start.1 = (bf16[127,1024]{1,0:T(8,128)(2,1)S(1)}, bf16[127,1024]{1,0:T(8,128)(2,1)S(1)}, u32[]{:S(2)}, u32[]{:S(2)}) collective-permute-start(bf16[127,1024]{1,0:T(8,128)(2,1)S(1)} %slice_bitcast_fusion.2), channel_id=1, source_target_pairs={{0,8},{8,16},{16,24},{24,32},{32,40},{40,48},{48,56},{56,64},{64,7... | collective-permute-start | bytes 780296 | tf_op jit(solution)/shard_map/ppermute | solution.py:10
  367.0 2.8 copy-start.5
Sparse Core Ops, SparseCore 0:
  369.9 254.3 all-reduce.2
where the time goes:
time: 633 us; the launch traced here: 632 us
  blocking collectives  295 us (47%)
  waiting for transfers between devices  252 us (40%)
  matrix products  46 us (7%)
  between operations  15.1 us (2%)
  local copies, waits for them, and re-layouts  12.5 us (2%)
  starting transfers between devices  8.34 us (1%)
    psum x1, blocking collectives, body(): grad_short = lax.psum(short_part, 'seq')  278 us
    unnamed x2, waiting for transfers between devices  239 us
    conv_general_dilated x6, matrix products, depthwise(): lax.conv_general_dilated(extended[None], kernel, (1,), [(0, 0)], dimensio...  46 us
    all_to_all x1, blocking collectives, body(): lax.all_to_all(grad_output, 'chan', split_axis=1, concat_axis=0, tiled=True)  16.3 us
  transfers between devices with their start and end apart: 5, of which 3 were waited for; matrix products, arithmetic and copies ran while one was open for 3% of the time, Pallas kernels for 0%

commit v1 on v0

v1 whole, which is shorter than its diff:
```python
import functools

import jax
import jax.numpy as jnp
from jax import lax
from jax.experimental import pallas as pl
from jax.experimental.pallas import tpu as pltpu
from jax.sharding import PartitionSpec as P

MESH = pl.DeviceIdType.MESH
NX, NZ = 4, 16


def passed_along(shard, axis, by):
    length = lax.axis_size(axis)
    pairs = [(i, i + by) for i in range(length) if 0 <= i + by < length]
    return lax.ppermute(shard, axis, pairs)


def depthwise(extended, kernel):
    channels = kernel.shape[2]
    result = lax.conv_general_dilated(
        extended[None],
        kernel,
        (1,),
        [(0, 0)],
        dimension_numbers=("NWC", "WIO", "NWC"),
        feature_group_count=channels,
        preferred_element_type=jnp.float32,
    )
    return result[0]


def causal_apply(extended, weights):
    return depthwise(extended, jnp.flip(weights, 0)[:, None, :])


def forward_apply(extended, weights):
    return depthwise(extended, weights[:, None, :])


def filter_partial(history, grad):
    return jnp.flip(depthwise(history, grad[:, None, :]), 0)


def reduce_kernel(
    long_ref, short_ref, long_out, short_out,
    send_a, recv_a, send_s, recv_s, acc, send_z, recv_z, gath,
    sem_sa, sem_ra, sem_ss, sem_rs, sem_sz, sem_rz, sem_sg, sem_rg,
):
    seq = lax.axis_index("seq")
    chan = lax.axis_index("chan")
    x = seq // NZ
    z = seq % NZ

    def at_x(d):
        return ((x + d) % NX) * NZ + z

    def at_z(d):
        return x * NZ + (z + d) % NZ

    barrier = pltpu.get_barrier_semaphore()
    for d in range(1, NX):
        pl.semaphore_signal(barrier, inc=1, device_id=(at_x(d), chan), device_id_type=MESH)
    for d in range(1, NZ):
        pl.semaphore_signal(barrier, inc=1, device_id=(at_z(d), chan), device_id_type=MESH)
    for k in range(NX):
        send_a[k] = long_ref[32 * k : 32 * k + 32, :].astype(jnp.bfloat16)
        send_s[k] = short_ref[:, 256 * k : 256 * k + 256]
    pl.semaphore_wait(barrier, NX + NZ - 2)

    copies = []
    for d in range(1, NX):
        to = (x + d) % NX
        for src, dst, ss, rs in ((send_a, recv_a, sem_sa, sem_ra), (send_s, recv_s, sem_ss, sem_rs)):
            copy = pltpu.make_async_remote_copy(
                src_ref=src.at[to], dst_ref=dst.at[d - 1],
                send_sem=ss.at[d - 1], recv_sem=rs.at[d - 1],
                device_id=(at_x(d), chan), device_id_type=MESH,
            )
            copy.start()
            copies.append(copy)
    total = long_ref[pl.ds(pl.multiple_of(x * 32, 32), 32), :]
    stotal = send_s[x]
    for copy in copies:
        copy.wait()
    for d in range(1, NX):
        total = total + recv_a[d - 1].astype(jnp.float32)
        stotal = stotal + recv_s[d - 1]
    acc[...] = total
    tail = jnp.concatenate(
        [
            jnp.concatenate([stotal[r : r + 1] for r in range(4 * h, 4 * h + 4)], axis=1)
            for h in range(2)
        ],
        axis=0,
    )
    for k in range(NZ):
        send_z[k] = jnp.concatenate([acc[2 * k : 2 * k + 2, :], tail], axis=0).astype(jnp.bfloat16)
    copies = []
    for d in range(1, NZ):
        copy = pltpu.make_async_remote_copy(
            src_ref=send_z.at[(z + d) % NZ], dst_ref=recv_z.at[z],
            send_sem=sem_sz.at[d - 1], recv_sem=sem_rz.at[d - 1],
            device_id=(at_z(d), chan), device_id_type=MESH,
        )
        copy.start()
        copies.append(copy)
    recv_z[z] = send_z[z]
    for copy in copies:
        copy.wait()
    both = recv_z[0].astype(jnp.float32)
    for k in range(1, NZ):
        both = both + recv_z[k].astype(jnp.float32)
    long_out[...] = both[0:2]
    mine = jnp.concatenate(
        [both[2 + r // 4 : 3 + r // 4, 256 * (r % 4) : 256 * (r % 4) + 256] for r in range(8)], axis=0
    )
    gath[x] = mine
    copies = []
    for d in range(1, NX):
        copy = pltpu.make_async_remote_copy(
            src_ref=gath.at[x], dst_ref=gath.at[x],
            send_sem=sem_sg.at[d - 1], recv_sem=sem_rg.at[d - 1],
            device_id=(at_x(d), chan), device_id_type=MESH,
        )
        copy.start()
        copies.append(copy)
    for copy in copies:
        copy.wait()
    for k in range(NX):
        short_out[:, 256 * k : 256 * k + 256] = gath[k]


def reduce_both(long_part, short_part):
    chans = long_part.shape[1]
    vmem = pl.BlockSpec(memory_space=pltpu.VMEM)
    dma = pltpu.SemaphoreType.DMA
    return pl.pallas_call(
        reduce_kernel,
        out_shape=(
            jax.ShapeDtypeStruct((2, chans), jnp.float32),
            jax.ShapeDtypeStruct((8, chans), jnp.float32),
        ),
        in_specs=[vmem, vmem],
        out_specs=(vmem, vmem),
        scratch_shapes=[
            pltpu.VMEM((NX, 32, chans), jnp.bfloat16),
            pltpu.VMEM((NX - 1, 32, chans), jnp.bfloat16),
            pltpu.VMEM((NX, 8, chans // NX), jnp.float32),
            pltpu.VMEM((NX - 1, 8, chans // NX), jnp.float32),
            pltpu.VMEM((32, chans), jnp.float32),
            pltpu.VMEM((NZ, 4, chans), jnp.bfloat16),
            pltpu.VMEM((NZ, 4, chans), jnp.bfloat16),
            pltpu.VMEM((NX, 8, chans // NX), jnp.float32),
            dma((NX - 1,)), dma((NX - 1,)), dma((NX - 1,)), dma((NX - 1,)),
            dma((NZ - 1,)), dma((NZ - 1,)), dma((NX - 1,)), dma((NX - 1,)),
        ],
        compiler_params=pltpu.CompilerParams(collective_id=1, has_side_effects=True),
        name="reduce_both",
    )(long_part, short_part)


def body(key_gate, values, query_gate, grad_output, short_taps, long_taps):
    long_len = long_taps.shape[0]
    short_len = short_taps.shape[0]
    halo = long_len + short_len - 2
    row_count = key_gate.shape[0]
    product = (key_gate.astype(jnp.float32) * values.astype(jnp.float32)).astype(jnp.bfloat16)
    before = passed_along(product[row_count - halo :], "seq", 1)
    cotangent = lax.all_to_all(grad_output, "chan", split_axis=1, concat_axis=0, tiled=True)
    grad_mixed = (cotangent.astype(jnp.float32) * query_gate.astype(jnp.float32)).astype(
        jnp.bfloat16
    )
    after = passed_along(grad_mixed[:halo], "seq", -1)
    product_ext = jnp.concatenate([before, product], 0)
    long_ext = causal_apply(product_ext, short_taps).astype(jnp.bfloat16)
    mixed = causal_apply(long_ext, long_taps)
    grad_query = (cotangent.astype(jnp.float32) * mixed).astype(jnp.bfloat16)
    long_back = jnp.concatenate([grad_mixed, after], 0)
    short_back = forward_apply(long_back, long_taps).astype(jnp.bfloat16)
    grad_product = forward_apply(short_back, short_taps)
    grad_key = (grad_product * values.astype(jnp.float32)).astype(jnp.bfloat16)
    grad_value = (grad_product * key_gate.astype(jnp.float32)).astype(jnp.bfloat16)
    long_part = filter_partial(long_ext, grad_mixed)
    short_part = filter_partial(product_ext[long_len - 1 :], short_back[:row_count])
    short_part = jnp.pad(short_part, ((0, 1), (0, 0)))
    grad_long, grad_short = reduce_both(long_part, short_part)
    return (grad_query, grad_key, grad_value, grad_long, grad_short[:short_len])


def solution(mesh):
    in_specs = (
        P("seq", "chan"),
        P("seq", "chan"),
        P("seq", "chan"),
        P(("seq", "chan"), None),
        P(None, "chan"),
        P(None, "chan"),
    )
    out_specs = (
        P("seq", "chan"),
        P("seq", "chan"),
        P("seq", "chan"),
        P("seq", "chan"),
        P(None, "chan"),
    )
    return jax.shard_map(body, mesh=mesh, in_specs=in_specs, out_specs=out_specs, check_vma=False)
```

time: 633 us -> 137 us (0.22)
  blocking collectives: 295 us -> 16.3 us
  waiting for transfers between devices: 252 us -> 9.72 us
  Pallas kernels: 0 us -> 36 us
  between operations: 15.1 us -> 0.92 us
    psum x1 -> x0, blocking collectives: 278 us -> none  [body(): grad_short = lax.psum(short_part, 'seq')]
    unnamed x2 -> x0, waiting for transfers between devices: 239 us -> none
    pallas_call x0 -> x1, Pallas kernels: none -> 36 us  [reduce_both(): pl.pallas_call(reduce_kernel, out_shape=(jax.ShapeDtypeStruct((2, chans),...]
  transfers between devices with their start and end apart: 5 -> 2, of which waited for: 3 -> 2; matrix products, arithmetic and copies ran while one was open for 3% -> 3% of each run, Pallas kernels for 0% -> 0%
where the time goes in v1:
time: 137 us; the launch traced here: 136 us
  matrix products  50.5 us (37%)
  Pallas kernels  36 us (26%)
  blocking collectives  16.3 us (12%)
  local copies, waits for them, and re-layouts  15.1 us (11%)
  waiting for transfers between devices  9.72 us (7%)
  other arithmetic  4.14 us (3%)
  starting transfers between devices  3.2 us (2%)
    conv_general_dilated x6, matrix products, depthwise(): lax.conv_general_dilated(extended[None], kernel, (1,), [(0, 0)], dimensio...  50.5 us
    pallas_call x1, Pallas kernels, reduce_both(): pl.pallas_call(reduce_kernel, out_shape=(jax.ShapeDtypeStruct((2, chans),...  36 us
    all_to_all x1, blocking collectives, body(): lax.all_to_all(grad_output, 'chan', split_axis=1, concat_axis=0, tiled=True)  16.3 us
    ppermute x2, waiting for transfers between devices, passed_along(): return lax.ppermute(shard, axis, pairs)  9.72 us
    rev x2, local copies, waits for them, and re-layouts, causal_apply(): return depthwise(extended, jnp.flip(weights, 0)[:, None, :])  3.42 us
    ppermute x2, starting transfers between devices, passed_along(): return lax.ppermute(shard, axis, pairs)  3.2 us
    convert_element_type x1, local copies, waits for them, and re-layouts, body(): short_back = forward_apply(long_back, long_taps).astype(jnp.bfloat16)  3.18 us
    rev x2, local copies, waits for them, and re-layouts, filter_partial(): return jnp.flip(depthwise(history, grad[:, None, :]), 0)  2.83 us
  transfers between devices with their start and end apart: 2, of which 2 were waited for; matrix products, arithmetic and copies ran while one was open for 3% of the time, Pallas kernels for 0%

profile of v1, /device:TPU:24, one launch (start us, length us, event | category | flops | bytes accessed | tf_op | source)
XLA Modules:
  0.0 135.9 jit_solution(16081456610577128275)
XLA Ops:
  0.6 1.1 copy.75
  1.8 16.3 %all_to_all.13 = bf16[32,8,1024]{2,0,1:T(8,128)(2,1)S(1)} all-to-all(bf16[32,8,1024]{2,0,1:T(8,128)(2,1)S(1)} %bitcast.49), channel_id=1, replica_groups=mesh['seq'=64,'chan'=8] {'chan'}, dimensions={1} | all-to-all | bytes 1048576 | tf_op jit(solution)/shard_map/all_to_all | solution.py:171
  18.3 1.4 %collective-permute-start.1 = (bf16[133,1024]{1,0:T(8,128)(2,1)S(1)}, bf16[133,1024]{1,0:T(8,128)(2,1)S(1)}, u32[]{:S(2)}, u32[]{:S(2)}) collective-permute-start(bf16[133,1024]{1,0:T(8,128)(2,1)S(1)} %slice.24), channel_id=1, source_target_pairs={{8,0},{16,8},{24,16},{32,24},{40,32},{48,40},{56,48},{64,56},{72,6... | collective-permute-start | bytes 817160 | tf_op jit(solution)/shard_map/ppermute | solution.py:17
  19.8 8.6 %collective-permute-done.1 = bf16[133,1024]{1,0:T(8,128)(2,1)S(1)} collective-permute-done((bf16[133,1024]{1,0:T(8,128)(2,1)S(1)}, bf16[133,1024]{1,0:T(8,128)(2,1)S(1)}, u32[]{:S(2)}, u32[]{:S(2)}) %collective-permute-start.1) | collective-permute-done | bytes 272416 | tf_op jit(solution)/shard_map/ppermute | solution.py:17
  28.5 14.4 %fusion.8 = bf16[1,262,1024]{2,0,1:T(2,128)(2,1)S(1)} fusion(bf16[1,389,1024]{2,1,0:T(8,128)(2,1)S(1)} %maximum_bitcast_fusion, bf16[128,1,1024]{2,0,1:T(8,128)(2,1)S(1)} %bitcast.51), kind=kOutput, calls=%fused_computation.9 | convolution fusion | flops 68950016 | bytes 1595392 | tf_op jit(solution)/shard_map/conv_general_dilated | solution.py:22
  42.9 1.0 copy-done
  43.9 3.2 %pad_reduce_fusion = bf16[264,1024]{1,0:T(8,128)(2,1)S(1)} fusion(bf16[1,262,1024]{2,0,1:T(2,128)(2,1)S(1)} %fusion.8), kind=kLoop, calls=%fused_computation.15 | loop fusion | bytes 1077248 | tf_op jit(solution)/shard_map/convert_element_type | solution.py:181
  47.3 0.3 copy.42
  47.8 0.6 convolution_select_fusion
  48.4 0.6 copy.44
  49.2 2.6 %fusion.14 = (bf16[256,1024]{1,0:T(8,128)(2,1)}, bf16[256,1024]{1,0:T(8,128)(2,1)}, bf16[256,1024]{1,0:T(8,128)(2,1)S(1)}) fusion(bf16[256,1024]{1,0:T(8,128)(2,1)} %param.6, f32[1,264,1024]{2,1,0:T(8,128)S(1)} %reshape.24, bf16[256,1024]{1,0:T(8,128)(2,1)} %param.7), kind=kLoop, calls=%fused_computation.18 | loop fusion | flops 2097152 | bytes 3670016 | tf_op jit(solution)/shard_map/convert_element_type | solution.py:184
  51.8 1.8 %collective-permute-start = (bf16[133,1024]{1,0:T(8,128)(2,1)S(1)}, bf16[133,1024]{1,0:T(8,128)(2,1)S(1)}, u32[]{:S(2)}, u32[]{:S(2)}) collective-permute-start(bf16[133,1024]{1,0:T(8,128)(2,1)S(1)} %slice.23), channel_id=1, source_target_pairs={{0,8},{8,16},{16,24},{24,32},{32,40},{40,48},{48,56},{56,64},{64,7... | collective-permute-start | bytes 817160 | tf_op jit(solution)/shard_map/ppermute | solution.py:17
  53.8 3.2 %rev.17 = bf16[128,1024]{1,0:T(8,128)(2,1)S(1)} reverse(bf16[128,1024]{1,0:T(8,128)(2,1)} %param.11), dimensions={0} | reverse | bytes 524288 | tf_op jit(solution)/shard_map/jit(_flip)/rev | solution.py:35
  57.0 1.1 collective-permute-done
  58.3 2.5 %fusion.12 = f32[1,7,1024]{2,0,1:T(1,128)S(1)} fusion(bf16[1,262,1024]{2,1,0:T(8,128)(2,1)S(1)} %fusion.28, bf16[1,262,1024]{2,0,1:T(2,128)(2,1)S(1)} %copy-done.1), kind=kOutput, calls=%fused_computation.16 | convolution fusion | flops 3670016 | bytes 1617920 | tf_op jit(solution)/shard_map/conv_general_dilated | solution.py:22
  61.2 3.2 %fusion.2 = bf16[1,383,1024]{2,0,1:T(2,128)(2,1)S(1)} fusion(bf16[1,389,1024]{2,1,0:T(8,128)(2,1)S(1)} %fusion.20, bf16[7,1,1024]{2,0,1:T(8,128)(2,1)S(1)} %bitcast.56), kind=kOutput, calls=%fused_computation.2 | convolution fusion | flops 5490688 | bytes 1595392 | tf_op jit(solution)/shard_map/conv_general_dilated | solution.py:22
  64.4 14.1 %fusion.4 = f32[1,128,1024]{2,0,1:T(1,128)S(1)} fusion(bf16[1,383,1024]{2,0,1:T(2,128)(2,1)S(1)} %fusion.2, bf16[256,1,1024]{2,0,1:T(8,128)(2,1)S(1)} %bitcast.47), kind=kOutput, calls=%fused_computation.4 | convolution fusion | flops 67108864 | bytes 1832960 | tf_op jit(solution)/shard_map/conv_general_dilated | solution.py:22
  78.6 2.6 %rev.18.long_ref = f32[128,1024]{1,0:T(8,128)} reverse(f32[128,1024]{1,0:T(8,128)S(1)} %bitcast.48), dimensions={0} | reverse | bytes 1048576 | tf_op jit(solution)/shard_map/jit(_flip)/rev | solution.py:43
  81.2 0.6 pad.4.short_ref
  81.8 36.0 %reduce_both.1 = (f32[2,1024]{1,0:T(2,128)}, f32[8,1024]{1,0:T(8,128)}) custom-call(f32[128,1024]{1,0:T(8,128)} %rev.18.long_ref, f32[8,1024]{1,0:T(8,128)} %pad.4.short_ref), custom_call_target="tpu_custom_call" | custom-call | tf_op jit(solution)/shard_map/reduce_both/pallas_call | solution.py:139
  117.8 15.7 %fusion.6 = f32[1,256,1024]{2,0,1:T(1,128)S(1)} fusion(bf16[1,383,1024]{2,0,1:T(2,128)(2,1)} %copy-done.8, bf16[128,1,1024]{2,0,1:T(8,128)(2,1)S(1)} %bitcast.52), kind=kOutput, calls=%fused_computation.6 | convolution fusion | flops 67108864 | bytes 2095104 | tf_op jit(solution)/shard_map/conv_general_dilated | solution.py:22
  133.6 1.1 fusion.17
  134.6 0.6 copy.80
  135.2 0.6 copy.81
  (30 shorter events, 1.7 us)
Async XLA Ops:
  0.6 17.5 %copy-start.2 = (bf16[256,1024]{1,0:T(8,128)(2,1)S(1)}, bf16[256,1024]{1,0:T(8,128)(2,1)}, u32[]{:S(2)}) copy-start(bf16[256,1024]{1,0:T(8,128)(2,1)} %param.8) | copy-start | bytes 1572868
  18.3 10.2 %copy-start.3 = (bf16[128,1024]{1,0:T(8,128)(2,1)S(1)}, bf16[128,1024]{1,0:T(8,128)(2,1)}, u32[]{:S(2)}) copy-start(bf16[128,1024]{1,0:T(8,128)(2,1)} %param.11) | copy-start | bytes 786436
  18.3 10.1 %collective-permute-start.1 = (bf16[133,1024]{1,0:T(8,128)(2,1)S(1)}, bf16[133,1024]{1,0:T(8,128)(2,1)S(1)}, u32[]{:S(2)}, u32[]{:S(2)}) collective-permute-start(bf16[133,1024]{1,0:T(8,128)(2,1)S(1)} %slice.24), channel_id=1, source_target_pairs={{8,0},{16,8},{24,16},{32,24},{40,32},{48,40},{56,48},{64,56},{72,6... | collective-permute-start | bytes 817160 | tf_op jit(solution)/shard_map/ppermute | solution.py:17
  42.9 1.0 copy-start
  47.0 0.7 copy-start.5
  47.1 0.7 copy-start.7
  51.7 6.5 %copy-start.1 = (bf16[1,262,1024]{2,0,1:T(2,128)(2,1)S(1)}, bf16[1,262,1024]{2,0,1:T(2,128)(2,1)}, u32[]{:S(2)}) copy-start(bf16[1,262,1024]{2,0,1:T(2,128)(2,1)} %copy-done) | copy-start | bytes 1609732
  51.8 6.3 %collective-permute-start = (bf16[133,1024]{1,0:T(8,128)(2,1)S(1)}, bf16[133,1024]{1,0:T(8,128)(2,1)S(1)}, u32[]{:S(2)}, u32[]{:S(2)}) collective-permute-start(bf16[133,1024]{1,0:T(8,128)(2,1)S(1)} %slice.23), channel_id=1, source_target_pairs={{0,8},{8,16},{16,24},{24,32},{32,40},{40,48},{48,56},{56,64},{64,7... | collective-permute-start | bytes 817160 | tf_op jit(solution)/shard_map/ppermute | solution.py:17
  64.4 14.1 %copy-start.8 = (bf16[1,383,1024]{2,0,1:T(2,128)(2,1)}, bf16[1,383,1024]{2,0,1:T(2,128)(2,1)S(1)}, u32[]{:S(2)}) copy-start(bf16[1,383,1024]{2,0,1:T(2,128)(2,1)S(1)} %fusion.2) | copy-start | bytes 2353156
  133.5 1.1 copy-start.6
  133.6 1.7 %copy-start.4 = (f32[8,1024]{1,0:T(8,128)S(1)}, f32[8,1024]{1,0:T(8,128)}, u32[]{:S(2)}) copy-start(f32[8,1024]{1,0:T(8,128)} %get-tuple-element.8) | copy-start | bytes 98308

commit v2 on v0

v2 whole, which is shorter than its diff:
```python
import jax
import jax.numpy as jnp
from jax import lax
from jax.experimental import pallas as pl
from jax.experimental.pallas import tpu as pltpu
from jax.sharding import PartitionSpec as P

MESH = pl.DeviceIdType.MESH
NX, NZ, NC = 4, 16, 8
NSEQ = NX * NZ
HALO = 144
LANES = 128

F32 = jnp.float32
BF16 = jnp.bfloat16


def remote(src, dst, send, recv, device):
    return pltpu.make_async_remote_copy(
        src_ref=src, dst_ref=dst, send_sem=send, recv_sem=recv,
        device_id=device, device_id_type=MESH,
    )


def kernel(
    key_ref, val_ref, query_ref, go_ref, st_ref, lt_ref,
    gq_ref, gk_ref, gv_ref, long_out, short_out,
    cot, send_p, halo_p, send_g, halo_g, ext, gext, soext, shifted, gshift, mixed, gs,
    lp, send_a, recv_a, send_z, recv_z, sp, send_s, recv_s, send_t, recv_t, gath,
    sem_own, sem_c, rem_c, sem_p, rem_p, sem_g, rem_g, sem_a, rem_a, sem_z, rem_z,
    sem_s, rem_s, sem_t, rem_t, sem_h, rem_h,
):
    rows, chans = key_ref.shape
    groups = chans // LANES
    short_len = st_ref.shape[0]
    seq = lax.axis_index("seq")
    chan = lax.axis_index("chan")
    x = seq // NZ
    z = seq % NZ
    following = (seq + 1) % NSEQ
    preceding = (seq + NSEQ - 1) % NSEQ

    def at_x(d):
        return ((x + d) % NX) * NZ + z

    def at_z(d):
        return x * NZ + (z + d) % NZ

    def lanes(c):
        return pl.ds(pl.multiple_of(c * LANES, LANES), LANES)

    barrier = pltpu.get_barrier_semaphore()
    peers = [(seq, (chan + d) % NC) for d in range(1, NC)]
    peers += [(following, chan), (preceding, chan)]
    peers += [(at_x(d), chan) for d in range(1, NX)] + [(at_z(d), chan) for d in range(1, NZ)]
    for peer in peers:
        pl.semaphore_signal(barrier, inc=1, device_id=peer, device_id_type=MESH)

    def gate(c, carry):
        product = (key_ref[:, lanes(c)].astype(F32) * val_ref[:, lanes(c)].astype(F32)).astype(BF16)
        send_p[:, lanes(c)] = product[rows - HALO :]
        ext[c, HALO:, :] = product.astype(F32)
        return carry

    lax.fori_loop(0, groups, gate, 0)
    pl.semaphore_wait(barrier, len(peers))

    own = pltpu.make_async_copy(
        go_ref.at[:, pl.ds(pl.multiple_of(chan * chans, chans), chans)], cot.at[chan], sem_own
    )
    own.start()
    tokens = []
    for d in range(1, NC):
        to = (chan + d) % NC
        tokens.append(
            remote(
                go_ref.at[:, pl.ds(pl.multiple_of(to * chans, chans), chans)], cot.at[chan],
                sem_c.at[d - 1], rem_c.at[d - 1], (seq, to),
            )
        )
    for copy in tokens:
        copy.start()
    ahead = remote(send_p, halo_p, sem_p, rem_p, (following, chan))
    ahead.start()

    def short_rows(c, low, high):
        total = jnp.zeros((high - low, LANES), F32)
        for i in range(short_len):
            tap = st_ref[i : i + 1, lanes(c)].astype(F32)
            total = total + tap * ext[c, low + 16 - i : high + 16 - i, :]
        return total.astype(BF16).astype(F32)

    def long_tile(c, table, start, size, sign):
        def taps(q, acc):
            eight = lt_ref[pl.ds(pl.multiple_of(q * 8, 8), 8), lanes(c)]
            at = pl.multiple_of(start + sign * q * 8, 8)
            for s in range(8):
                acc = acc + eight[s : s + 1] * table[c, s, pl.ds(at, size), :]
            return acc

        return lax.fori_loop(0, 16, taps, jnp.zeros((size, LANES), F32))

    def later(c, carry):
        soext[136:384, :] = short_rows(c, 136, 384)
        for s in range(8):
            shifted[c, s, 144:384, :] = soext[144 - s : 384 - s, :]
        mixed[136:256, lanes(c)] = long_tile(c, shifted, 264, 120, -1)
        return carry

    lax.fori_loop(0, groups, later, 0)
    ahead.wait()

    def earlier(c, carry):
        ext[c, :HALO, :] = jnp.where(seq > 0, halo_p[:, lanes(c)].astype(F32), 0.0)
        soext[0:144, :] = short_rows(c, 0, 144)
        for s in range(8):
            shifted[c, s, 8:144, :] = soext[8 - s : 144 - s, :]
        mixed[0:136, lanes(c)] = long_tile(c, shifted, 128, 136, -1)
        return carry

    lax.fori_loop(0, groups, earlier, 0)
    own.wait()
    for copy in tokens:
        copy.wait()

    def outer(c, carry):
        got = cot[:, :, lanes(c)].reshape(rows, LANES).astype(F32)
        product = (got * query_ref[:, lanes(c)].astype(F32)).astype(BF16)
        send_g[:, lanes(c)] = product[:HALO]
        gext[c, :rows, :] = product.astype(F32)
        gq_ref[:, lanes(c)] = (got * mixed[:, lanes(c)]).astype(BF16)
        return carry

    lax.fori_loop(0, groups, outer, 0)
    back = remote(send_g, halo_g, sem_g, rem_g, (preceding, chan))
    back.start()

    def correlate(c, carry):
        def lags(q, inner):
            sums = [jnp.zeros((8, LANES), F32) for _ in range(8)]
            for part in range(4):
                grads = gext[c, 64 * part : 64 * part + 64, :]
                at = pl.multiple_of(128 + 64 * part - q * 8, 8)
                for s in range(8):
                    terms = grads * shifted[c, s, pl.ds(at, 64), :]
                    sums[s] = sums[s] + jnp.sum(terms.reshape(8, 8, LANES), axis=0)
            lp[pl.ds(pl.multiple_of(q * 8, 8), 8), lanes(c)] = jnp.concatenate(
                [jnp.sum(item, axis=0, keepdims=True) for item in sums], axis=0
            )
            return inner

        return lax.fori_loop(0, 16, lags, carry)

    lax.fori_loop(0, groups, correlate, 0)
    for k in range(NX):
        send_a[k] = lp[32 * k : 32 * k + 32, :].astype(BF16)
    back.wait()

    def backward(c, carry):
        gext[c, rows:, :] = jnp.where(seq < NSEQ - 1, halo_g[:, lanes(c)].astype(F32), 0.0)
        for s in range(8):
            gshift[c, s, :, :] = gext[c, s : s + 384, :]
        gs[0:128, :] = long_tile(c, gshift, 0, 128, 1).astype(BF16).astype(F32)
        gs[128:264, :] = long_tile(c, gshift, 128, 136, 1).astype(BF16).astype(F32)
        total = jnp.zeros((rows, LANES), F32)
        sums = []
        here = gs[0:rows, :]
        for i in range(short_len):
            tap = st_ref[i : i + 1, lanes(c)].astype(F32)
            total = total + tap * gs[i : i + rows, :]
            sums.append(jnp.sum(here * ext[c, HALO - i : HALO - i + rows, :], axis=0, keepdims=True))
        sums.append(jnp.zeros((1, LANES), F32))
        sp[:, lanes(c)] = jnp.concatenate(sums, axis=0)
        gk_ref[:, lanes(c)] = (total * val_ref[:, lanes(c)].astype(F32)).astype(BF16)
        gv_ref[:, lanes(c)] = (total * key_ref[:, lanes(c)].astype(F32)).astype(BF16)
        return carry

    first = [
        remote(send_a.at[(x + d) % NX], recv_a.at[d - 1], sem_a.at[d - 1], rem_a.at[d - 1], (at_x(d), chan))
        for d in range(1, NX)
    ]
    for copy in first:
        copy.start()
    lax.fori_loop(0, groups // 2, backward, 0)
    for copy in first:
        copy.wait()
    summed = lp[pl.ds(pl.multiple_of(x * 32, 32), 32), :]
    for d in range(1, NX):
        summed = summed + recv_a[d - 1].astype(F32)
    lp[0:32, :] = summed
    for k in range(NZ):
        send_z[k] = lp[2 * k : 2 * k + 2, :].astype(BF16)
    second = [
        remote(send_z.at[(z + d) % NZ], recv_z.at[d - 1], sem_z.at[d - 1], rem_z.at[d - 1], (at_z(d), chan))
        for d in range(1, NZ)
    ]
    for copy in second:
        copy.start()
    lax.fori_loop(groups // 2, groups, backward, 0)

    width = chans // NX
    for k in range(NX):
        send_s[k] = sp[:, width * k : width * k + width]
    third = [
        remote(send_s.at[(x + d) % NX], recv_s.at[d - 1], sem_s.at[d - 1], rem_s.at[d - 1], (at_x(d), chan))
        for d in range(1, NX)
    ]
    for copy in third:
        copy.start()
    for copy in second:
        copy.wait()
    both = send_z[z].astype(F32)
    for d in range(1, NZ):
        both = both + recv_z[d - 1].astype(F32)
    long_out[...] = both
    for copy in third:
        copy.wait()
    mine = send_s[x]
    for d in range(1, NX):
        mine = mine + recv_s[d - 1]
    send_t[...] = mine.astype(BF16)
    fourth = [
        remote(send_t, recv_t.at[z], sem_t.at[d - 1], rem_t.at[d - 1], (at_z(d), chan))
        for d in range(1, NZ)
    ]
    for copy in fourth:
        copy.start()
    recv_t[z] = mine.astype(BF16)
    for copy in fourth:
        copy.wait()
    mine = recv_t[0].astype(F32)
    for k in range(1, NZ):
        mine = mine + recv_t[k].astype(F32)
    gath[x] = mine
    fifth = [
        remote(gath.at[x], gath.at[x], sem_h.at[d - 1], rem_h.at[d - 1], (at_x(d), chan))
        for d in range(1, NX)
    ]
    for copy in fifth:
        copy.start()
    for copy in fifth:
        copy.wait()
    for k in range(NX):
        short_out[:, width * k : width * k + width] = gath[k]


def body(key_gate, values, query_gate, grad_output, short_taps, long_taps):
    rows, chans = key_gate.shape
    groups = chans // LANES
    width = chans // NX
    vmem = pl.BlockSpec(memory_space=pltpu.VMEM)
    dma = pltpu.SemaphoreType.DMA
    V = pltpu.VMEM
    grad_query, grad_key, grad_value, grad_long, grad_short = pl.pallas_call(
        kernel,
        out_shape=(
            jax.ShapeDtypeStruct((rows, chans), BF16),
            jax.ShapeDtypeStruct((rows, chans), BF16),
            jax.ShapeDtypeStruct((rows, chans), BF16),
            jax.ShapeDtypeStruct((2, chans), F32),
            jax.ShapeDtypeStruct((8, chans), F32),
        ),
        in_specs=[vmem, vmem, vmem, pl.BlockSpec(memory_space=pl.ANY), vmem, vmem],
        out_specs=(vmem,) * 5,
        scratch_shapes=[
            V((NC, rows // NC, chans), BF16),
            V((HALO, chans), BF16), V((HALO, chans), BF16),
            V((HALO, chans), BF16), V((HALO, chans), BF16),
            V((groups, HALO + rows, LANES), F32), V((groups, HALO + rows, LANES), F32),
            V((384, LANES), F32),
            V((groups, 8, 384, LANES), F32), V((groups, 8, 384, LANES), F32),
            V((rows, chans), F32), V((264, LANES), F32),
            V((128, chans), F32),
            V((NX, 32, chans), BF16), V((NX - 1, 32, chans), BF16),
            V((NZ, 2, chans), BF16), V((NZ - 1, 2, chans), BF16),
            V((8, chans), F32), V((NX, 8, width), F32), V((NX - 1, 8, width), F32),
            V((8, width), BF16), V((NZ, 8, width), BF16), V((NX, 8, width), F32),
            dma, dma((NC - 1,)), dma((NC - 1,)), dma, dma, dma, dma,
            dma((NX - 1,)), dma((NX - 1,)), dma((NZ - 1,)), dma((NZ - 1,)),
            dma((NX - 1,)), dma((NX - 1,)), dma((NZ - 1,)), dma((NZ - 1,)),
            dma((NX - 1,)), dma((NX - 1,)),
        ],
        compiler_params=pltpu.CompilerParams(
            collective_id=1, has_side_effects=True, vmem_limit_bytes=60 * 1024 * 1024
        ),
        name="conv_chain",
    )(key_gate, values, query_gate, grad_output, short_taps, long_taps.astype(F32))
    return (grad_query, grad_key, grad_value, grad_long, grad_short[: short_taps.shape[0]])


def solution(mesh):
    in_specs = (
        P("seq", "chan"),
        P("seq", "chan"),
        P("seq", "chan"),
        P(("seq", "chan"), None),
        P(None, "chan"),
        P(None, "chan"),
    )
    out_specs = (
        P("seq", "chan"),
        P("seq", "chan"),
        P("seq", "chan"),
        P("seq", "chan"),
        P(None, "chan"),
    )
    return jax.shard_map(body, mesh=mesh, in_specs=in_specs, out_specs=out_specs, check_vma=False)
```

time: 633 us -> 80.5 us (0.13)
  blocking collectives: 295 us -> 0 us
  waiting for transfers between devices: 252 us -> 0 us
  Pallas kernels: 0 us -> 72.6 us
  matrix products: 46 us -> 0 us
  between operations: 15.1 us -> 0.65 us
  starting transfers between devices: 8.34 us -> 0 us
  local copies, waits for them, and re-layouts: 12.5 us -> 5.17 us
    psum x1 -> x0, blocking collectives: 278 us -> none  [body(): grad_short = lax.psum(short_part, 'seq')]
    unnamed x2 -> x0, waiting for transfers between devices: 239 us -> none
    pallas_call x0 -> x1, Pallas kernels: none -> 72.6 us  [body(): pl.pallas_call(kernel, out_shape=(jax.ShapeDtypeStruct((rows, chans), BF1...]
    conv_general_dilated x6 -> x0, matrix products: 46 us -> none  [depthwise(): lax.conv_general_dilated(extended[None], kernel, (1,), [(0, 0)], dimensio...]
    all_to_all x1 -> x0, blocking collectives: 16.3 us -> none  [body(): lax.all_to_all(grad_output, 'chan', split_axis=1, concat_axis=0, tiled=True)]
    ppermute x4 -> x0, waiting for transfers between devices: 12.4 us -> none  [passed_along(): return lax.ppermute(shard, axis, pairs)]
    ppermute x4 -> x0, starting transfers between devices: 8.3 us -> none  [passed_along(): return lax.ppermute(shard, axis, pairs)]
  transfers between devices with their start and end apart: 5 -> 0, of which waited for: 3 -> 0; matrix products, arithmetic and copies ran while one was open for 3% -> 0% of each run, Pallas kernels for 0% -> 0%
where the time goes in v2:
time: 80.5 us; the launch traced here: 80.2 us
  Pallas kernels  72.6 us (90%)
  local copies, waits for them, and re-layouts  5.17 us (6%)
  other arithmetic  1.79 us (2%)
    pallas_call x1, Pallas kernels, body(): pl.pallas_call(kernel, out_shape=(jax.ShapeDtypeStruct((rows, chans), BF1...  72.6 us
    unnamed x13, local copies, waits for them, and re-layouts  5.17 us
    convert_element_type x1, other arithmetic, body(): long_taps.astype(F32)  1.79 us

profile of v2, /device:TPU:24, one launch (start us, length us, event | category | flops | bytes accessed | tf_op | source)
XLA Modules:
  0.0 80.2 jit_solution(1313352640452970212)
XLA Ops:
  0.6 1.8 %convert_element_type.3.lt_ref = f32[128,1024]{1,0:T(8,128)} convert(bf16[128,1024]{1,0:T(8,128)(2,1)} %param.11) | non-fusion elementwise | flops 131072 | bytes 786432 | tf_op jit(solution)/shard_map/convert_element_type | solution.py:287
  2.4 72.6 %conv_chain.1 = (bf16[256,1024]{1,0:T(8,128)(2,1)}, bf16[256,1024]{1,0:T(8,128)(2,1)}, bf16[256,1024]{1,0:T(8,128)(2,1)}, f32[2,1024]{1,0:T(2,128)}, f32[8,1024]{1,0:T(8,128)}) custom-call(bf16[256,1024]{1,0:T(8,128)(2,1)} %key_ref.1, bf16[256,1024]{1,0:T(8,128)(2,1)} %val_ref.1, bf16[256,1024]{1,0:T(8,128)(2,1)} %query_ref.1, bf16[32,8192]{1,0:T(8,128)(2,1)} %go_ref.1, ...), custom_call_target="tpu_custom_call" | custom-call | tf_op jit(solution)/shard_map/conv_chain/pallas_call | solution.py:254
  75.0 0.0 copy-start.1
  75.0 1.9 %copy.16 = bf16[256,1024]{1,0:T(8,128)(2,1)} copy(bf16[256,1024]{1,0:T(8,128)(2,1)} %get-tuple-element.20) | data formatting | bytes 1048576
  77.0 0.0 copy-done.1
  77.0 0.0 copy-start
  77.0 0.8 copy.17
  77.8 0.4 copy-done
  78.2 0.0 copy-start.3
  78.2 0.0 copy-start.2
  78.2 0.8 copy.18
  79.0 0.0 copy-done.3
  79.0 0.6 copy.19
  79.6 0.0 copy-done.2
  79.6 0.6 copy.20
Async XLA Ops:
  75.0 1.9 %copy-start.1 = (bf16[256,1024]{1,0:T(8,128)(2,1)S(1)}, bf16[256,1024]{1,0:T(8,128)(2,1)}, u32[]{:S(2)}) copy-start(bf16[256,1024]{1,0:T(8,128)(2,1)} %get-tuple-element.21) | copy-start | bytes 1572868
  77.0 1.2 %copy-start = (bf16[256,1024]{1,0:T(8,128)(2,1)S(1)}, bf16[256,1024]{1,0:T(8,128)(2,1)}, u32[]{:S(2)}) copy-start(bf16[256,1024]{1,0:T(8,128)(2,1)} %get-tuple-element.22) | copy-start | bytes 1572868
  78.2 0.8 copy-start.3
  78.2 1.4 %copy-start.2 = (f32[8,1024]{1,0:T(8,128)S(1)}, f32[8,1024]{1,0:T(8,128)}, u32[]{:S(2)}) copy-start(f32[8,1024]{1,0:T(8,128)} %get-tuple-element.14) | copy-start | bytes 98308

commit v3 on v2

--- a/solution.py
+++ b/solution.py
@@ -25,7 +25,7 @@
 def kernel(
     key_ref, val_ref, query_ref, go_ref, st_ref, lt_ref,
     gq_ref, gk_ref, gv_ref, long_out, short_out,
-    cot, send_p, halo_p, send_g, halo_g, ext, gext, soext, shifted, gshift, mixed, gs,
+    ltf, cot, send_p, halo_p, send_g, halo_g, ext, gext, soext, shifted, gshift, mixed, gs,
     lp, send_a, recv_a, send_z, recv_z, sp, send_s, recv_s, send_t, recv_t, gath,
     sem_own, sem_c, rem_c, sem_p, rem_p, sem_g, rem_g, sem_a, rem_a, sem_z, rem_z,
     sem_s, rem_s, sem_t, rem_t, sem_h, rem_h,
@@ -55,6 +55,8 @@
     peers += [(at_x(d), chan) for d in range(1, NX)] + [(at_z(d), chan) for d in range(1, NZ)]
     for peer in peers:
         pl.semaphore_signal(barrier, inc=1, device_id=peer, device_id_type=MESH)
+
+    ltf[...] = lt_ref[...].astype(F32)
 
     def gate(c, carry):
         product = (key_ref[:, lanes(c)].astype(F32) * val_ref[:, lanes(c)].astype(F32)).astype(BF16)
@@ -92,7 +94,7 @@
 
     def long_tile(c, table, start, size, sign):
         def taps(q, acc):
-            eight = lt_ref[pl.ds(pl.multiple_of(q * 8, 8), 8), lanes(c)]
+            eight = ltf[pl.ds(pl.multiple_of(q * 8, 8), 8), lanes(c)]
             at = pl.multiple_of(start + sign * q * 8, 8)
             for s in range(8):
                 acc = acc + eight[s : s + 1] * table[c, s, pl.ds(at, size), :]
@@ -110,15 +112,14 @@
     lax.fori_loop(0, groups, later, 0)
     ahead.wait()
 
-    def earlier(c, carry):
+    def history(c, carry):
         ext[c, :HALO, :] = jnp.where(seq > 0, halo_p[:, lanes(c)].astype(F32), 0.0)
         soext[0:144, :] = short_rows(c, 0, 144)
         for s in range(8):
             shifted[c, s, 8:144, :] = soext[8 - s : 144 - s, :]
-        mixed[0:136, lanes(c)] = long_tile(c, shifted, 128, 136, -1)
-        return carry
-
-    lax.fori_loop(0, groups, earlier, 0)
+        return carry
+
+    lax.fori_loop(0, groups, history, 0)
     own.wait()
     for copy in tokens:
         copy.wait()
@@ -128,7 +129,6 @@
         product = (got * query_ref[:, lanes(c)].astype(F32)).astype(BF16)
         send_g[:, lanes(c)] = product[:HALO]
         gext[c, :rows, :] = product.astype(F32)
-        gq_ref[:, lanes(c)] = (got * mixed[:, lanes(c)]).astype(BF16)
         return carry
 
     lax.fori_loop(0, groups, outer, 0)
@@ -198,6 +198,12 @@
         copy.start()
     lax.fori_loop(groups // 2, groups, backward, 0)
 
+    def finish(c, carry):
+        mixed[0:136, lanes(c)] = long_tile(c, shifted, 128, 136, -1)
+        got = cot[:, :, lanes(c)].reshape(rows, LANES).astype(F32)
+        gq_ref[:, lanes(c)] = (got * mixed[:, lanes(c)]).astype(BF16)
+        return carry
+
     width = chans // NX
     for k in range(NX):
         send_s[k] = sp[:, width * k : width * k + width]
@@ -213,6 +219,7 @@
     for d in range(1, NZ):
         both = both + recv_z[d - 1].astype(F32)
     long_out[...] = both
+    lax.fori_loop(0, 2, finish, 0)
     for copy in third:
         copy.wait()
     mine = send_s[x]
@@ -226,6 +233,7 @@
     for copy in fourth:
         copy.start()
     recv_t[z] = mine.astype(BF16)
+    lax.fori_loop(2, groups - 1, finish, 0)
     for copy in fourth:
         copy.wait()
     mine = recv_t[0].astype(F32)
@@ -238,6 +246,7 @@
     ]
     for copy in fifth:
         copy.start()
+    lax.fori_loop(groups - 1, groups, finish, 0)
     for copy in fifth:
         copy.wait()
     for k in range(NX):
@@ -263,6 +272,7 @@
         in_specs=[vmem, vmem, vmem, pl.BlockSpec(memory_space=pl.ANY), vmem, vmem],
         out_specs=(vmem,) * 5,
         scratch_shapes=[
+            V(long_taps.shape, F32),
             V((NC, rows // NC, chans), BF16),
             V((HALO, chans), BF16), V((HALO, chans), BF16),
             V((HALO, chans), BF16), V((HALO, chans), BF16),
@@ -284,7 +294,7 @@
             collective_id=1, has_side_effects=True, vmem_limit_bytes=60 * 1024 * 1024
         ),
         name="conv_chain",
-    )(key_gate, values, query_gate, grad_output, short_taps, long_taps.astype(F32))
+    )(key_gate, values, query_gate, grad_output, short_taps, long_taps)
     return (grad_query, grad_key, grad_value, grad_long, grad_short[: short_taps.shape[0]])
 
 

time: 80.5 us -> 74.1 us (0.920); the launches traced: 80.2 us -> 72.8 us
  Pallas kernels: 72.6 us -> 66.9 us
  other arithmetic: 1.79 us -> 0 us
    pallas_call x1, Pallas kernels: 72.6 us -> 66.9 us  [body(): pl.pallas_call(kernel, out_shape=(jax.ShapeDtypeStruct((rows, chans), BF1...]
    convert_element_type x1 -> x0, other arithmetic: 1.79 us -> none  [body(): long_taps.astype(F32)]
where the time goes in v3:
time: 74.1 us; the launch traced here: 72.8 us
  Pallas kernels  66.9 us (90%)
  local copies, waits for them, and re-layouts  5.17 us (7%)
    pallas_call x1, Pallas kernels, body(): pl.pallas_call(kernel, out_shape=(jax.ShapeDtypeStruct((rows, chans), BF1...  66.9 us
    unnamed x13, local copies, waits for them, and re-layouts  5.17 us

profile of v3, /device:TPU:24, one launch (start us, length us, event | category | flops | bytes accessed | tf_op | source)
XLA Modules:
  0.0 72.8 jit_solution(6930377857341923777)
XLA Ops:
  0.6 66.9 %conv_chain.1 = (bf16[256,1024]{1,0:T(8,128)(2,1)}, bf16[256,1024]{1,0:T(8,128)(2,1)}, bf16[256,1024]{1,0:T(8,128)(2,1)}, f32[2,1024]{1,0:T(2,128)}, f32[8,1024]{1,0:T(8,128)}) custom-call(bf16[256,1024]{1,0:T(8,128)(2,1)} %key_ref.1, bf16[256,1024]{1,0:T(8,128)(2,1)} %val_ref.1, bf16[256,1024]{1,0:T(8,128)(2,1)} %query_ref.1, bf16[32,8192]{1,0:T(8,128)(2,1)} %go_ref.1, ...), custom_call_target="tpu_custom_call" | custom-call | tf_op jit(solution)/shard_map/conv_chain/pallas_call | solution.py:263
  67.6 0.0 copy-start.1
  67.6 1.9 %copy.16 = bf16[256,1024]{1,0:T(8,128)(2,1)} copy(bf16[256,1024]{1,0:T(8,128)(2,1)} %get-tuple-element.20) | data formatting | bytes 1048576
  69.5 0.0 copy-done.1
  69.5 0.0 copy-start
  69.5 0.8 %copy.17 = bf16[256,1024]{1,0:T(8,128)(2,1)} copy(bf16[256,1024]{1,0:T(8,128)(2,1)S(1)} %copy-done.1) | data formatting | bytes 1048576
  70.3 0.4 copy-done
  70.7 0.0 copy-start.3
  70.7 0.0 copy-start.2
  70.7 0.8 %copy.18 = bf16[256,1024]{1,0:T(8,128)(2,1)} copy(bf16[256,1024]{1,0:T(8,128)(2,1)S(1)} %copy-done) | data formatting | bytes 1048576
  71.5 0.0 copy-done.3
  71.5 0.6 copy.19
  72.1 0.0 copy-done.2
  72.1 0.6 copy.20
Async XLA Ops:
  67.6 1.9 %copy-start.1 = (bf16[256,1024]{1,0:T(8,128)(2,1)S(1)}, bf16[256,1024]{1,0:T(8,128)(2,1)}, u32[]{:S(2)}) copy-start(bf16[256,1024]{1,0:T(8,128)(2,1)} %get-tuple-element.21) | copy-start | bytes 1572868
  69.5 1.2 %copy-start = (bf16[256,1024]{1,0:T(8,128)(2,1)S(1)}, bf16[256,1024]{1,0:T(8,128)(2,1)}, u32[]{:S(2)}) copy-start(bf16[256,1024]{1,0:T(8,128)(2,1)} %get-tuple-element.22) | copy-start | bytes 1572868
  70.7 0.8 %copy-start.3 = (f32[2,1024]{1,0:T(2,128)S(1)}, f32[2,1024]{1,0:T(2,128)}, u32[]{:S(2)}) copy-start(f32[2,1024]{1,0:T(2,128)} %get-tuple-element.23) | copy-start | bytes 24580
  70.7 1.4 %copy-start.2 = (f32[8,1024]{1,0:T(8,128)S(1)}, f32[8,1024]{1,0:T(8,128)}, u32[]{:S(2)}) copy-start(f32[8,1024]{1,0:T(8,128)} %get-tuple-element.14) | copy-start | bytes 98308

commit v4 on v3

--- a/solution.py
+++ b/solution.py
@@ -13,6 +13,12 @@
 
 F32 = jnp.float32
 BF16 = jnp.bfloat16
+
+
+def tree(terms):
+    while len(terms) > 1:
+        terms = [terms[k] + terms[k + 1] for k in range(0, len(terms), 2)]
+    return terms[0]
 
 
 def remote(src, dst, send, recv, device):
@@ -94,19 +100,22 @@
 
     def long_tile(c, table, start, size, sign):
         def taps(q, acc):
-            eight = ltf[pl.ds(pl.multiple_of(q * 8, 8), 8), lanes(c)]
-            at = pl.multiple_of(start + sign * q * 8, 8)
-            for s in range(8):
-                acc = acc + eight[s : s + 1] * table[c, s, pl.ds(at, size), :]
-            return acc
-
-        return lax.fori_loop(0, 16, taps, jnp.zeros((size, LANES), F32))
+            some = ltf[pl.ds(pl.multiple_of(q * 16, 16), 16), lanes(c)]
+            at = start // 16 + sign * q
+            terms = []
+            for t in range(16):
+                tap = jnp.broadcast_to(some[t : t + 1], (16, LANES)).astype(BF16)
+                terms.append(tap[None] * table[c, t, pl.ds(at, size // 16)])
+            return acc + tree(terms[:8]).astype(F32) + tree(terms[8:]).astype(F32)
+
+        shape = (size // 16, 16, LANES)
+        return lax.fori_loop(0, 8, taps, jnp.zeros(shape, F32)).reshape(size, LANES)
 
     def later(c, carry):
         soext[136:384, :] = short_rows(c, 136, 384)
-        for s in range(8):
-            shifted[c, s, 144:384, :] = soext[144 - s : 384 - s, :]
-        mixed[136:256, lanes(c)] = long_tile(c, shifted, 264, 120, -1)
+        for s in range(16):
+            shifted[c, s, 10:24] = soext[160 - s : 384 - s, :].astype(BF16).reshape(14, 16, LANES)
+        mixed[144:256, lanes(c)] = long_tile(c, shifted, 272, 112, -1)
         return carry
 
     lax.fori_loop(0, groups, later, 0)
@@ -114,9 +123,9 @@
 
     def history(c, carry):
         ext[c, :HALO, :] = jnp.where(seq > 0, halo_p[:, lanes(c)].astype(F32), 0.0)
-        soext[0:144, :] = short_rows(c, 0, 144)
-        for s in range(8):
-            shifted[c, s, 8:144, :] = soext[8 - s : 144 - s, :]
+        soext[0:160, :] = short_rows(c, 0, 160)
+        for s in range(16):
+            shifted[c, s, 1:10] = soext[16 - s : 160 - s, :].astype(BF16).reshape(9, 16, LANES)
         return carry
 
     lax.fori_loop(0, groups, history, 0)
@@ -137,19 +146,18 @@
 
     def correlate(c, carry):
         def lags(q, inner):
-            sums = [jnp.zeros((8, LANES), F32) for _ in range(8)]
-            for part in range(4):
-                grads = gext[c, 64 * part : 64 * part + 64, :]
-                at = pl.multiple_of(128 + 64 * part - q * 8, 8)
-                for s in range(8):
-                    terms = grads * shifted[c, s, pl.ds(at, 64), :]
-                    sums[s] = sums[s] + jnp.sum(terms.reshape(8, 8, LANES), axis=0)
-            lp[pl.ds(pl.multiple_of(q * 8, 8), 8), lanes(c)] = jnp.concatenate(
+            sums = [jnp.zeros((16, LANES), F32) for _ in range(16)]
+            for part in range(2):
+                grads = gext[c, 128 * part : 128 * part + 128, :].astype(BF16).reshape(8, 16, LANES)
+                for t in range(16):
+                    terms = grads * shifted[c, t, pl.ds(8 + 8 * part - q, 8)]
+                    sums[t] = sums[t] + tree([terms[k] for k in range(8)]).astype(F32)
+            lp[pl.ds(pl.multiple_of(q * 16, 16), 16), lanes(c)] = jnp.concatenate(
                 [jnp.sum(item, axis=0, keepdims=True) for item in sums], axis=0
             )
             return inner
 
-        return lax.fori_loop(0, 16, lags, carry)
+        return lax.fori_loop(0, 8, lags, carry)
 
     lax.fori_loop(0, groups, correlate, 0)
     for k in range(NX):
@@ -158,10 +166,10 @@
 
     def backward(c, carry):
         gext[c, rows:, :] = jnp.where(seq < NSEQ - 1, halo_g[:, lanes(c)].astype(F32), 0.0)
-        for s in range(8):
-            gshift[c, s, :, :] = gext[c, s : s + 384, :]
+        for s in range(16):
+            gshift[c, s] = gext[c, s : s + 384, :].astype(BF16).reshape(24, 16, LANES)
         gs[0:128, :] = long_tile(c, gshift, 0, 128, 1).astype(BF16).astype(F32)
-        gs[128:264, :] = long_tile(c, gshift, 128, 136, 1).astype(BF16).astype(F32)
+        gs[128:272, :] = long_tile(c, gshift, 128, 144, 1).astype(BF16).astype(F32)
         total = jnp.zeros((rows, LANES), F32)
         sums = []
         here = gs[0:rows, :]
@@ -199,7 +207,7 @@
     lax.fori_loop(groups // 2, groups, backward, 0)
 
     def finish(c, carry):
-        mixed[0:136, lanes(c)] = long_tile(c, shifted, 128, 136, -1)
+        mixed[0:144, lanes(c)] = long_tile(c, shifted, 128, 144, -1)
         got = cot[:, :, lanes(c)].reshape(rows, LANES).astype(F32)
         gq_ref[:, lanes(c)] = (got * mixed[:, lanes(c)]).astype(BF16)
         return carry
@@ -278,8 +286,8 @@
             V((HALO, chans), BF16), V((HALO, chans), BF16),
             V((groups, HALO + rows, LANES), F32), V((groups, HALO + rows, LANES), F32),
             V((384, LANES), F32),
-            V((groups, 8, 384, LANES), F32), V((groups, 8, 384, LANES), F32),
-            V((rows, chans), F32), V((264, LANES), F32),
+            V((groups, 16, 24, 16, LANES), BF16), V((groups, 16, 24, 16, LANES), BF16),
+            V((rows, chans), F32), V((272, LANES), F32),
             V((128, chans), F32),
             V((NX, 32, chans), BF16), V((NX - 1, 32, chans), BF16),
             V((NZ, 2, chans), BF16), V((NZ - 1, 2, chans), BF16),

time: 74.1 us -> 68.8 us (0.928)
  the two profiles are of different devices: /device:TPU:24 before, /device:TPU:2 now
where the time goes in v4:
time: 68.8 us; the launch traced here: 68.5 us
  Pallas kernels  62.7 us (91%)
  local copies, waits for them, and re-layouts  5.17 us (8%)
    pallas_call x1, Pallas kernels, body(): pl.pallas_call(kernel, out_shape=(jax.ShapeDtypeStruct((rows, chans), BF1...  62.7 us
    unnamed x13, local copies, waits for them, and re-layouts  5.17 us

profile of v4, /device:TPU:2, one launch (start us, length us, event | category | flops | bytes accessed | tf_op | source)
XLA Modules:
  0.0 68.5 jit_solution(8033304132915562746)
XLA Ops:
  0.6 62.7 %conv_chain.1 = (bf16[256,1024]{1,0:T(8,128)(2,1)}, bf16[256,1024]{1,0:T(8,128)(2,1)}, bf16[256,1024]{1,0:T(8,128)(2,1)}, f32[2,1024]{1,0:T(2,128)}, f32[8,1024]{1,0:T(8,128)}) custom-call(bf16[256,1024]{1,0:T(8,128)(2,1)} %key_ref.1, bf16[256,1024]{1,0:T(8,128)(2,1)} %val_ref.1, bf16[256,1024]{1,0:T(8,128)(2,1)} %query_ref.1, bf16[32,8192]{1,0:T(8,128)(2,1)} %go_ref.1, ...), custom_call_target="tpu_custom_call" | custom-call | tf_op jit(solution)/shard_map/conv_chain/pallas_call | solution.py:271
  63.3 0.0 copy-start.1
  63.4 1.9 %copy.16 = bf16[256,1024]{1,0:T(8,128)(2,1)} copy(bf16[256,1024]{1,0:T(8,128)(2,1)} %get-tuple-element.20) | data formatting | bytes 1048576
  65.3 0.0 copy-done.1
  65.3 0.0 copy-start
  65.3 0.8 %copy.17 = bf16[256,1024]{1,0:T(8,128)(2,1)} copy(bf16[256,1024]{1,0:T(8,128)(2,1)S(1)} %copy-done.1) | data formatting | bytes 1048576
  66.1 0.4 copy-done
  66.5 0.0 copy-start.3
  66.5 0.0 copy-start.2
  66.5 0.8 %copy.18 = bf16[256,1024]{1,0:T(8,128)(2,1)} copy(bf16[256,1024]{1,0:T(8,128)(2,1)S(1)} %copy-done) | data formatting | bytes 1048576
  67.3 0.0 copy-done.3
  67.3 0.6 copy.19
  67.9 0.0 copy-done.2
  67.9 0.6 copy.20
Async XLA Ops:
  63.3 1.9 %copy-start.1 = (bf16[256,1024]{1,0:T(8,128)(2,1)S(1)}, bf16[256,1024]{1,0:T(8,128)(2,1)}, u32[]{:S(2)}) copy-start(bf16[256,1024]{1,0:T(8,128)(2,1)} %get-tuple-element.21) | copy-start | bytes 1572868
  65.3 1.2 %copy-start = (bf16[256,1024]{1,0:T(8,128)(2,1)S(1)}, bf16[256,1024]{1,0:T(8,128)(2,1)}, u32[]{:S(2)}) copy-start(bf16[256,1024]{1,0:T(8,128)(2,1)} %get-tuple-element.22) | copy-start | bytes 1572868
  66.5 0.8 %copy-start.3 = (f32[2,1024]{1,0:T(2,128)S(1)}, f32[2,1024]{1,0:T(2,128)}, u32[]{:S(2)}) copy-start(f32[2,1024]{1,0:T(2,128)} %get-tuple-element.23) | copy-start | bytes 24580
  66.5 1.4 %copy-start.2 = (f32[8,1024]{1,0:T(8,128)S(1)}, f32[8,1024]{1,0:T(8,128)}, u32[]{:S(2)}) copy-start(f32[8,1024]{1,0:T(8,128)} %get-tuple-element.14) | copy-start | bytes 98308
